TPU v7x, 512 devices: a whole 4x4x16 slice. The times are simulated.
512 devices in a mesh: rows: 64 (over z, y), cols: 8 (over x, core).
Axes of the slice: x: 4, y: 4, z: 16, core: 2. Of those that a mesh axis runs over, the one named last changes fastest.
Arguments:
- sens_base: bfloat16 [524288, 1024], P('rows', 'cols'), may hold values from -0.14157282 to 0.14157282
- design_field: float32 [512, 1024], P('rows'), may hold values from -3 to 3
- gradient: bfloat16 [512, 1024], P('rows'), may hold values from -6 to 6
- tile_index: int32 [1024], P('cols'), may hold values from 0 to 31
- type_codes: int32 [1024], P('cols'), may hold values from 0 to 2
Outputs:
- r_panels: float32 [512, 1024], P(None, 'cols')
- multipliers: float32 [512], replicated
Inputs may be any that keep to these rules, and one draw needn't show every extreme that they name: `tile_index`: each constraint names one support tile.
All inputs are finite; a program needn't handle non-finite values.
Results may differ from a plain program's by a relative error of at most 0.0003.
The roundings to bfloat16 on the way count: a program that leaves them out, or rounds other values in their place, can miss the bound.
Values may be sent and summed in bfloat16 or wider, within the bound.
A program may use at most 64 MiB of HBM per device.

v0:
```python
import math
import jax
import jax.numpy as jnp
from jax import lax
from jax.sharding import PartitionSpec as P

TILE = 128
PW = 256


def padded_2(cells, sides, width):
    for axis, dim in sides:
        count = lax.axis_size(axis)
        ends = count - 1
        head = lax.slice_in_dim(cells, 0, width, axis=dim)
        tail = lax.slice_in_dim(cells, cells.shape[dim] - width, cells.shape[dim], axis=dim)
        cells = jnp.concatenate(
            [
                lax.ppermute(tail, axis, [(i, (i + 1) % count) for i in range(ends)]),
                cells,
                lax.ppermute(head, axis, [((i + 1) % count, i) for i in range(ends)]),
            ],
            axis=dim,
        )
    return cells


def assemble(base_cols, tile_cols, type_cols, stencils, cell_tile):
    kinds_all = jnp.arange(3, dtype=jnp.int32)
    chooser = (type_cols[None, :] == kinds_all[:, None]).astype(jnp.float32)
    picked = lax.dot_general(
        stencils,
        chooser,
        (((0,), (0,)), ((), ())),
        precision=lax.Precision.HIGHEST,
        preferred_element_type=jnp.float32,
    )
    inside = cell_tile[:, None] == tile_cols[None, :]
    total = base_cols.astype(jnp.float32) + jnp.where(inside, picked / TILE, 0.0)
    return total.astype(jnp.bfloat16)


def matmul(left, right):
    return jnp.dot(left, right, precision=lax.Precision.HIGHEST, preferred_element_type=jnp.float32)


def small_factor(matrix):
    order = matrix.shape[0]
    positions = jnp.arange(order, dtype=jnp.int32)

    def column_step(index_col, carry):
        working, lower = carry
        column = lax.dynamic_slice_in_dim(working, index_col, 1, 1)[:, 0]
        pivot = jnp.sqrt(lax.dynamic_slice_in_dim(column, index_col, 1, 0)[0])
        column = jnp.where(positions >= index_col, column / pivot, 0.0)
        lower = jnp.where(positions[None, :] == index_col, column[:, None], lower)
        working = working - column[:, None] * column[None, :]
        return (working, lower)

    return lax.fori_loop(0, order, column_step, (matrix, jnp.zeros_like(matrix)))[1]


def small_inverse(lower):
    order = lower.shape[0]
    positions = jnp.arange(order, dtype=jnp.int32)
    right = jnp.eye(order, dtype=jnp.float32)

    def row_step(index_row, carry):
        rest, solved = carry
        column = lax.dynamic_slice_in_dim(lower, index_row, 1, 1)[:, 0]
        pivot = lax.dynamic_slice_in_dim(column, index_row, 1, 0)[0]
        value = lax.dynamic_slice_in_dim(rest, index_row, 1, 0) / pivot
        solved = jnp.where(positions[:, None] == index_row, value, solved)
        below = jnp.where(positions > index_row, column, 0.0)
        rest = rest - below[:, None] * value
        return (rest, solved)

    return lax.fori_loop(0, order, row_step, (right, jnp.zeros_like(right)))[1]


def factor_lower(matrix):
    order = matrix.shape[0]
    width = math.gcd(order, 32)
    working = matrix
    lower = jnp.zeros_like(matrix)
    inverses = []
    for block_num in range(order // width):
        start = block_num * width
        diag_lower = small_factor(working[:width, :width])
        diag_inverse = small_inverse(diag_lower)
        inverses.append(diag_inverse)
        lower = lower.at[start : start + width, start : start + width].set(diag_lower)
        if start + width < order:
            panel = matmul(working[width:, :width], diag_inverse.T)
            lower = lower.at[start + width :, start : start + width].set(panel)
            working = working[width:, width:] - matmul(panel, panel.T)
    return (lower, inverses)


def solve_forward(lower, inverses, right):
    width = inverses[0].shape[0]
    solved = []
    for block_num in range(len(inverses)):
        start = block_num * width
        rest = right[start : start + width]
        if block_num > 0:
            rest = rest - matmul(
                lower[start : start + width, :start], jnp.concatenate(solved, axis=0)
            )
        solved.append(matmul(inverses[block_num], rest))
    return jnp.concatenate(solved, axis=0)


def solve_backward(lower, inverses, right):
    width = inverses[0].shape[0]
    order = lower.shape[0]
    solved = []
    for block_num in reversed(range(len(inverses))):
        start = block_num * width
        rest = right[start : start + width]
        if start + width < order:
            rest = rest - matmul(
                lower[start + width :, start : start + width].T, jnp.concatenate(solved, axis=0)
            )
        solved.insert(0, matmul(inverses[block_num].T, rest))
    return jnp.concatenate(solved, axis=0)


def shards(sens_base, design_field, gradient, tile_index, type_codes):
    rows_here = design_field.shape[0]
    grid_width = design_field.shape[1]
    cols_here = sens_base.shape[1]
    factored = 2 * PW
    padded = padded_2(design_field, (("rows", 0),), 1)
    padded = jnp.pad(padded, ((0, 0), (1, 1)))
    north_cells = padded[:-2, 1:-1]
    south_cells = padded[2:, 1:-1]
    west_cells = padded[1:-1, :-2]
    east_cells = padded[1:-1, 2:]
    laplace = 4.0 * design_field - (north_cells + south_cells + west_cells + east_cells)
    slope_x = 0.5 * (east_cells - west_cells)
    slope_y = 0.5 * (south_cells - north_cells)
    stencils = jnp.stack([laplace, slope_x, slope_y]).reshape(3, -1)
    row_glob = lax.axis_index("rows") * rows_here + jnp.arange(rows_here, dtype=jnp.int32)
    col_ids = jnp.arange(grid_width, dtype=jnp.int32) // TILE
    cell_tile = ((row_glob // TILE)[:, None] * (grid_width // TILE) + col_ids[None, :]).reshape(-1)
    local_jac = assemble(sens_base, tile_index, type_codes, stencils, cell_tile)
    grad_flat = gradient.reshape(-1)
    row_major = lax.all_to_all(local_jac, "cols", split_axis=0, concat_axis=1, tiled=True)
    row_piece = row_major.shape[0]
    grad_part = lax.dynamic_slice_in_dim(
        grad_flat, lax.axis_index("cols") * row_piece, row_piece, 0
    )
    leading = row_major[:, :factored]
    gram_block = lax.dot_general(
        leading, row_major, (((0,), (0,)), ((), ())), preferred_element_type=jnp.float32
    )
    projected = jnp.dot(grad_part, leading, preferred_element_type=jnp.float32)
    gram_block, projected = lax.psum((gram_block, projected), ("rows", "cols"))
    gram_head = gram_block[:, :factored]
    gram_own = lax.dynamic_slice_in_dim(
        gram_block, lax.axis_index("cols") * cols_here, cols_here, 1
    )
    lower_chol, inverses = factor_lower(gram_head)
    r_panels = solve_forward(lower_chol, inverses, gram_own)
    half_solved = solve_forward(lower_chol, inverses, projected[:, None])
    multipliers = solve_backward(lower_chol, inverses, half_solved)[:, 0]
    return (r_panels, multipliers)


def solution(mesh):
    placed = (P("rows", "cols"), P("rows", None), P("rows", None), P("cols"), P("cols"))
    return jax.shard_map(
        shards, mesh=mesh, in_specs=placed, out_specs=(P(None, "cols"), P()), check_vma=False
    )
```

profile of v0, /device:TPU:1, one launch (start us, length us, event | category | flops | bytes accessed | tf_op | source)
XLA Modules:
  0.0 2140.8 jit_solution(14819654451309352459)
XLA Ops:
  68.0 110.2 %psum.15 = f32[512]{0:T(512)S(1)} all-reduce(f32[512]{0:T(512)S(1)} %bitcast.1236), channel_id=1, replica_groups=mesh['rows'=64,'cols'=8] {'rows','cols'}, use_global_device_ids=true, to_apply=%region_65.66 | all-reduce | flops 512 | bytes 4096 | tf_op jit(solution)/shard_map/psum | solution.py:159
  178.3 367.6 %all-reduce.4.cloned.1.call-done = f32[512,1024]{1,0:T(8,128)} async-done(((f32[512,1024]{1,0:T(8,128)}), f32[512,1024]{1,0:T(8,128)}) %all-reduce.4.cloned.1.call-update) | async-done | bytes 2097168 | tf_op jit(solution)/shard_map/psum | solution.py:159
  546.7 45.5 %while.671 = (s32[]{:T(128)}, f32[32,32]{0,1:T(8,128)S(1)}, f32[32,32]{0,1:T(8,128)S(1)}, s32[]{:T(128)}, s32[]{:T(128)}, /*index=5*/s32[]{:T(128)}) while((s32[]{:T(128)}, f32[32,32]{0,1:T(8,128)S(1)}, f32[32,32]{0,1:T(8,128)S(1)}, s32[]{:T(128)}, s32[]{:T(128)}, /*index=5*/s32[]{:T(128)}) %tuple.1741), condition=%wide.region_2.3_spmd.clone.clone, body=%wide.region_1.2_spmd.clone.clone.sunk | while | flops 4292 | bytes 19003 | solution.py:60
  639.5 45.0 %while.673 = (s32[]{:T(128)}, f32[32,32]{0,1:T(8,128)S(1)}, f32[32,32]{0,1:T(8,128)S(1)}, s32[]{:T(128)}, s32[]{:T(128)}, /*index=5*/s32[]{:T(128)}) while((s32[]{:T(128)}, f32[32,32]{0,1:T(8,128)S(1)}, f32[32,32]{0,1:T(8,128)S(1)}, s32[]{:T(128)}, s32[]{:T(128)}, /*index=5*/s32[]{:T(128)}) %tuple.1747), condition=%wide.region_6.7_spmd.clone.clone, body=%wide.region_5.6_spmd.clone.clone.sunk | while | flops 4292 | bytes 19003 | solution.py:60
  729.6 45.0 %while.675 = (s32[]{:T(128)}, f32[32,32]{0,1:T(8,128)S(1)}, f32[32,32]{0,1:T(8,128)S(1)}, s32[]{:T(128)}, s32[]{:T(128)}, /*index=5*/s32[]{:T(128)}) while((s32[]{:T(128)}, f32[32,32]{0,1:T(8,128)S(1)}, f32[32,32]{0,1:T(8,128)S(1)}, s32[]{:T(128)}, s32[]{:T(128)}, /*index=5*/s32[]{:T(128)}) %tuple.1753), condition=%wide.region_10.11_spmd.clone.clone, body=%wide.region_9.10_spmd.clone.clone.sunk | while | flops 4292 | bytes 19003 | solution.py:60
  774.6 43.6 %while.676 = (s32[]{:T(128)}, f32[32,32]{1,0:T(8,128)S(1)}, f32[32,32]{1,0:T(8,128)S(1)}, f32[32,32]{0,1:T(8,128)S(1)}, s32[]{:T(128)}, /*index=5*/s32[]{:T(128)}, s32[]{:T(128)}) while((s32[]{:T(128)}, f32[32,32]{1,0:T(8,128)S(1)}, f32[32,32]{1,0:T(8,128)S(1)}, f32[32,32]{0,1:T(8,128)S(1)}, s32[]{:T(128)}, ...), condition=%wide.region_12.13_spmd.clone.clone, body=%wide.region_11.12_spmd.clone.clone.sunk | while | flops 4228 | bytes 18367 | solution.py:78
  819.6 86.6 %while.677 = (s32[]{:T(128)}, f32[32,32]{0,1:T(8,128)S(1)}, f32[32,32]{0,1:T(8,128)}, s32[]{:T(128)}, s32[]{:T(128)}, /*index=5*/s32[]{:T(128)}) while((s32[]{:T(128)}, f32[32,32]{0,1:T(8,128)S(1)}, f32[32,32]{0,1:T(8,128)}, s32[]{:T(128)}, s32[]{:T(128)}, /*index=5*/s32[]{:T(128)}) %tuple.1759), condition=%wide.region_14.15_spmd.clone.clone, body=%wide.region_13.14_spmd.clone.clone.sunk | while | flops 4292 | bytes 19003 | solution.py:60
  917.0 86.4 %while.678 = (s32[]{:T(128)}, f32[32,32]{1,0:T(8,128)S(1)}, f32[32,32]{1,0:T(8,128)S(1)}, f32[32,32]{0,1:T(8,128)}, s32[]{:T(128)}, /*index=5*/s32[]{:T(128)}, s32[]{:T(128)}) while((s32[]{:T(128)}, f32[32,32]{1,0:T(8,128)S(1)}, f32[32,32]{1,0:T(8,128)S(1)}, f32[32,32]{0,1:T(8,128)}, s32[]{:T(128)}, ...), condition=%wide.region_16.17_spmd.clone.clone, body=%wide.region_15.16_spmd.clone.clone.sunk | while | flops 4228 | bytes 18751 | solution.py:78
  1004.5 45.0 %while.679 = (s32[]{:T(128)}, f32[32,32]{0,1:T(8,128)S(1)}, f32[32,32]{0,1:T(8,128)S(1)}, s32[]{:T(128)}, s32[]{:T(128)}, /*index=5*/s32[]{:T(128)}) while((s32[]{:T(128)}, f32[32,32]{0,1:T(8,128)S(1)}, f32[32,32]{0,1:T(8,128)S(1)}, s32[]{:T(128)}, s32[]{:T(128)}, /*index=5*/s32[]{:T(128)}) %tuple.1856), condition=%wide.region_18.19_spmd.clone.clone, body=%wide.region_17.18_spmd.clone.clone.sunk | while | flops 4292 | bytes 19003 | solution.py:60
  1049.5 43.6 %while.680 = (s32[]{:T(128)}, f32[32,32]{1,0:T(8,128)S(1)}, f32[32,32]{1,0:T(8,128)S(1)}, f32[32,32]{0,1:T(8,128)S(1)}, s32[]{:T(128)}, /*index=5*/s32[]{:T(128)}, s32[]{:T(128)}) while((s32[]{:T(128)}, f32[32,32]{1,0:T(8,128)S(1)}, f32[32,32]{1,0:T(8,128)S(1)}, f32[32,32]{0,1:T(8,128)S(1)}, s32[]{:T(128)}, ...), condition=%wide.region_20.21_spmd.clone.clone, body=%wide.region_19.20_spmd.clone.clone.sunk | while | flops 4228 | bytes 18367 | solution.py:78
  1094.1 45.0 %while.681 = (s32[]{:T(128)}, f32[32,32]{0,1:T(8,128)S(1)}, f32[32,32]{0,1:T(8,128)S(1)}, s32[]{:T(128)}, s32[]{:T(128)}, /*index=5*/s32[]{:T(128)}) while((s32[]{:T(128)}, f32[32,32]{0,1:T(8,128)S(1)}, f32[32,32]{0,1:T(8,128)S(1)}, s32[]{:T(128)}, s32[]{:T(128)}, /*index=5*/s32[]{:T(128)}) %tuple.1855), condition=%wide.region_22.23_spmd.clone.clone, body=%wide.region_21.22_spmd.clone.clone.sunk | while | flops 4292 | bytes 19003 | solution.py:60
  1139.2 43.6 %while.682 = (s32[]{:T(128)}, f32[32,32]{1,0:T(8,128)S(1)}, f32[32,32]{1,0:T(8,128)S(1)}, f32[32,32]{0,1:T(8,128)S(1)}, s32[]{:T(128)}, /*index=5*/s32[]{:T(128)}, s32[]{:T(128)}) while((s32[]{:T(128)}, f32[32,32]{1,0:T(8,128)S(1)}, f32[32,32]{1,0:T(8,128)S(1)}, f32[32,32]{0,1:T(8,128)S(1)}, s32[]{:T(128)}, ...), condition=%wide.region_24.25_spmd.clone.clone, body=%wide.region_23.24_spmd.clone.clone.sunk | while | flops 4228 | bytes 18367 | solution.py:78
  1183.8 45.0 %while.683 = (s32[]{:T(128)}, f32[32,32]{0,1:T(8,128)S(1)}, f32[32,32]{0,1:T(8,128)S(1)}, s32[]{:T(128)}, s32[]{:T(128)}, /*index=5*/s32[]{:T(128)}) while((s32[]{:T(128)}, f32[32,32]{0,1:T(8,128)S(1)}, f32[32,32]{0,1:T(8,128)S(1)}, s32[]{:T(128)}, s32[]{:T(128)}, /*index=5*/s32[]{:T(128)}) %tuple.1854), condition=%wide.region_26.27_spmd.clone.clone, body=%wide.region_25.26_spmd.clone.clone.sunk | while | flops 4292 | bytes 19003 | solution.py:60
  1228.8 43.6 %while.684 = (s32[]{:T(128)}, f32[32,32]{1,0:T(8,128)S(1)}, f32[32,32]{1,0:T(8,128)S(1)}, f32[32,32]{0,1:T(8,128)S(1)}, s32[]{:T(128)}, /*index=5*/s32[]{:T(128)}, s32[]{:T(128)}) while((s32[]{:T(128)}, f32[32,32]{1,0:T(8,128)S(1)}, f32[32,32]{1,0:T(8,128)S(1)}, f32[32,32]{0,1:T(8,128)S(1)}, s32[]{:T(128)}, ...), condition=%wide.region_28.29_spmd.clone.clone, body=%wide.region_27.28_spmd.clone.clone.sunk | while | flops 4228 | bytes 18367 | solution.py:78
  1273.3 45.0 %while.685 = (s32[]{:T(128)}, f32[32,32]{0,1:T(8,128)S(1)}, f32[32,32]{0,1:T(8,128)S(1)}, s32[]{:T(128)}, s32[]{:T(128)}, /*index=5*/s32[]{:T(128)}) while((s32[]{:T(128)}, f32[32,32]{0,1:T(8,128)S(1)}, f32[32,32]{0,1:T(8,128)S(1)}, s32[]{:T(128)}, s32[]{:T(128)}, /*index=5*/s32[]{:T(128)}) %tuple.1853), condition=%wide.region_30.31_spmd.clone.clone, body=%wide.region_29.30_spmd.clone.clone.sunk | while | flops 4292 | bytes 19003 | solution.py:60
  1326.6 43.6 %while.686 = (s32[]{:T(128)}, f32[32,32]{1,0:T(8,128)S(1)}, f32[32,32]{1,0:T(8,128)S(1)}, f32[32,32]{0,1:T(8,128)S(1)}, s32[]{:T(128)}, /*index=5*/s32[]{:T(128)}, s32[]{:T(128)}) while((s32[]{:T(128)}, f32[32,32]{1,0:T(8,128)S(1)}, f32[32,32]{1,0:T(8,128)S(1)}, f32[32,32]{0,1:T(8,128)S(1)}, s32[]{:T(128)}, ...), condition=%wide.region_32.33_spmd.clone.clone, body=%wide.region_31.32_spmd.clone.clone.sunk | while | flops 4228 | bytes 18367 | solution.py:78
  1371.0 45.0 %while.687 = (s32[]{:T(128)}, f32[32,32]{0,1:T(8,128)S(1)}, f32[32,32]{0,1:T(8,128)S(1)}, s32[]{:T(128)}, s32[]{:T(128)}, /*index=5*/s32[]{:T(128)}) while((s32[]{:T(128)}, f32[32,32]{0,1:T(8,128)S(1)}, f32[32,32]{0,1:T(8,128)S(1)}, s32[]{:T(128)}, s32[]{:T(128)}, /*index=5*/s32[]{:T(128)}) %tuple.1789), condition=%wide.region_34.35_spmd.clone.clone, body=%wide.region_33.34_spmd.clone.clone.sunk | while | flops 4292 | bytes 19003 | solution.py:60
  1416.1 43.6 %while.688 = (s32[]{:T(128)}, f32[32,32]{1,0:T(8,128)S(1)}, f32[32,32]{1,0:T(8,128)S(1)}, f32[32,32]{0,1:T(8,128)S(1)}, s32[]{:T(128)}, /*index=5*/s32[]{:T(128)}, s32[]{:T(128)}) while((s32[]{:T(128)}, f32[32,32]{1,0:T(8,128)S(1)}, f32[32,32]{1,0:T(8,128)S(1)}, f32[32,32]{0,1:T(8,128)S(1)}, s32[]{:T(128)}, ...), condition=%wide.region_36.37_spmd.clone.clone, body=%wide.region_35.36_spmd.clone.clone.sunk | while | flops 4228 | bytes 18367 | solution.py:78
  1460.5 45.0 %while.689 = (s32[]{:T(128)}, f32[32,32]{0,1:T(8,128)S(1)}, f32[32,32]{0,1:T(8,128)S(1)}, s32[]{:T(128)}, s32[]{:T(128)}, /*index=5*/s32[]{:T(128)}) while((s32[]{:T(128)}, f32[32,32]{0,1:T(8,128)S(1)}, f32[32,32]{0,1:T(8,128)S(1)}, s32[]{:T(128)}, s32[]{:T(128)}, /*index=5*/s32[]{:T(128)}) %tuple.1795), condition=%wide.region_38.39_spmd.clone.clone, body=%wide.region_37.38_spmd.clone.clone.sunk | while | flops 4292 | bytes 19003 | solution.py:60
  1505.5 43.6 %while.690 = (s32[]{:T(128)}, f32[32,32]{1,0:T(8,128)S(1)}, f32[32,32]{1,0:T(8,128)S(1)}, f32[32,32]{0,1:T(8,128)S(1)}, s32[]{:T(128)}, /*index=5*/s32[]{:T(128)}, s32[]{:T(128)}) while((s32[]{:T(128)}, f32[32,32]{1,0:T(8,128)S(1)}, f32[32,32]{1,0:T(8,128)S(1)}, f32[32,32]{0,1:T(8,128)S(1)}, s32[]{:T(128)}, ...), condition=%wide.region_40.41_spmd.clone.clone, body=%wide.region_39.40_spmd.clone.clone.sunk | while | flops 4228 | bytes 18367 | solution.py:78
  1549.8 45.0 %while.691 = (s32[]{:T(128)}, f32[32,32]{0,1:T(8,128)S(1)}, f32[32,32]{0,1:T(8,128)S(1)}, s32[]{:T(128)}, s32[]{:T(128)}, /*index=5*/s32[]{:T(128)}) while((s32[]{:T(128)}, f32[32,32]{0,1:T(8,128)S(1)}, f32[32,32]{0,1:T(8,128)S(1)}, s32[]{:T(128)}, s32[]{:T(128)}, /*index=5*/s32[]{:T(128)}) %tuple.1801), condition=%wide.region_42.43_spmd.clone.clone, body=%wide.region_41.42_spmd.clone.clone.sunk | while | flops 4292 | bytes 19003 | solution.py:60
  1594.9 43.6 %while.692 = (s32[]{:T(128)}, f32[32,32]{1,0:T(8,128)S(1)}, f32[32,32]{1,0:T(8,128)S(1)}, f32[32,32]{0,1:T(8,128)S(1)}, s32[]{:T(128)}, /*index=5*/s32[]{:T(128)}, s32[]{:T(128)}) while((s32[]{:T(128)}, f32[32,32]{1,0:T(8,128)S(1)}, f32[32,32]{1,0:T(8,128)S(1)}, f32[32,32]{0,1:T(8,128)S(1)}, s32[]{:T(128)}, ...), condition=%wide.region_44.45_spmd.clone.clone, body=%wide.region_43.44_spmd.clone.clone.sunk | while | flops 4228 | bytes 18367 | solution.py:78
  1639.2 45.0 %while.693 = (s32[]{:T(128)}, f32[32,32]{0,1:T(8,128)S(1)}, f32[32,32]{0,1:T(8,128)S(1)}, s32[]{:T(128)}, s32[]{:T(128)}, /*index=5*/s32[]{:T(128)}) while((s32[]{:T(128)}, f32[32,32]{0,1:T(8,128)S(1)}, f32[32,32]{0,1:T(8,128)S(1)}, s32[]{:T(128)}, s32[]{:T(128)}, /*index=5*/s32[]{:T(128)}) %tuple.1807), condition=%wide.region_46.47_spmd.clone.clone, body=%wide.region_45.46_spmd.clone.clone.sunk | while | flops 4292 | bytes 19003 | solution.py:60
  1691.8 43.6 %while.694 = (s32[]{:T(128)}, f32[32,32]{1,0:T(8,128)S(1)}, f32[32,32]{1,0:T(8,128)S(1)}, f32[32,32]{0,1:T(8,128)S(1)}, s32[]{:T(128)}, /*index=5*/s32[]{:T(128)}, s32[]{:T(128)}) while((s32[]{:T(128)}, f32[32,32]{1,0:T(8,128)S(1)}, f32[32,32]{1,0:T(8,128)S(1)}, f32[32,32]{0,1:T(8,128)S(1)}, s32[]{:T(128)}, ...), condition=%wide.region_48.49_spmd.clone.clone, body=%wide.region_47.48_spmd.clone.clone.sunk | while | flops 4228 | bytes 18367 | solution.py:78
  1736.0 45.0 %while.695 = (s32[]{:T(128)}, f32[32,32]{0,1:T(8,128)S(1)}, f32[32,32]{0,1:T(8,128)S(1)}, s32[]{:T(128)}, s32[]{:T(128)}, /*index=5*/s32[]{:T(128)}) while((s32[]{:T(128)}, f32[32,32]{0,1:T(8,128)S(1)}, f32[32,32]{0,1:T(8,128)S(1)}, s32[]{:T(128)}, s32[]{:T(128)}, /*index=5*/s32[]{:T(128)}) %tuple.1813), condition=%wide.region_50.51_spmd.clone.clone, body=%wide.region_49.50_spmd.clone.clone.sunk | while | flops 4292 | bytes 19003 | solution.py:60
  1781.0 43.6 %while.696 = (s32[]{:T(128)}, f32[32,32]{1,0:T(8,128)S(1)}, f32[32,32]{1,0:T(8,128)S(1)}, f32[32,32]{0,1:T(8,128)S(1)}, s32[]{:T(128)}, /*index=5*/s32[]{:T(128)}, s32[]{:T(128)}) while((s32[]{:T(128)}, f32[32,32]{1,0:T(8,128)S(1)}, f32[32,32]{1,0:T(8,128)S(1)}, f32[32,32]{0,1:T(8,128)S(1)}, s32[]{:T(128)}, ...), condition=%wide.region_52.53_spmd.clone.clone, body=%wide.region_51.52_spmd.clone.clone.sunk | while | flops 4228 | bytes 18367 | solution.py:78
  1825.1 45.0 %while.697 = (s32[]{:T(128)}, f32[32,32]{0,1:T(8,128)S(1)}, f32[32,32]{0,1:T(8,128)S(1)}, s32[]{:T(128)}, s32[]{:T(128)}, /*index=5*/s32[]{:T(128)}) while((s32[]{:T(128)}, f32[32,32]{0,1:T(8,128)S(1)}, f32[32,32]{0,1:T(8,128)S(1)}, s32[]{:T(128)}, s32[]{:T(128)}, /*index=5*/s32[]{:T(128)}) %tuple.1819), condition=%wide.region_54.55_spmd.clone.clone, body=%wide.region_53.54_spmd.clone.clone.sunk | while | flops 4292 | bytes 19003 | solution.py:60
  1870.2 43.6 %while.698 = (s32[]{:T(128)}, f32[32,32]{1,0:T(8,128)S(1)}, f32[32,32]{1,0:T(8,128)S(1)}, f32[32,32]{0,1:T(8,128)S(1)}, s32[]{:T(128)}, /*index=5*/s32[]{:T(128)}, s32[]{:T(128)}) while((s32[]{:T(128)}, f32[32,32]{1,0:T(8,128)S(1)}, f32[32,32]{1,0:T(8,128)S(1)}, f32[32,32]{0,1:T(8,128)S(1)}, s32[]{:T(128)}, ...), condition=%wide.region_56.57_spmd.clone.clone, body=%wide.region_55.56_spmd.clone.clone.sunk | while | flops 4228 | bytes 18367 | solution.py:78
  1914.3 45.0 %while.699 = (s32[]{:T(128)}, f32[32,32]{0,1:T(8,128)S(1)}, f32[32,32]{0,1:T(8,128)S(1)}, s32[]{:T(128)}, s32[]{:T(128)}, /*index=5*/s32[]{:T(128)}) while((s32[]{:T(128)}, f32[32,32]{0,1:T(8,128)S(1)}, f32[32,32]{0,1:T(8,128)S(1)}, s32[]{:T(128)}, s32[]{:T(128)}, /*index=5*/s32[]{:T(128)}) %tuple.1825), condition=%wide.region_58.59_spmd.clone.clone, body=%wide.region_57.58_spmd.clone.clone.sunk | while | flops 4292 | bytes 19003 | solution.py:60
  1959.4 43.6 %while.700 = (s32[]{:T(128)}, f32[32,32]{1,0:T(8,128)S(1)}, f32[32,32]{1,0:T(8,128)S(1)}, f32[32,32]{0,1:T(8,128)S(1)}, s32[]{:T(128)}, /*index=5*/s32[]{:T(128)}, s32[]{:T(128)}) while((s32[]{:T(128)}, f32[32,32]{1,0:T(8,128)S(1)}, f32[32,32]{1,0:T(8,128)S(1)}, f32[32,32]{0,1:T(8,128)S(1)}, s32[]{:T(128)}, ...), condition=%wide.region_60.61_spmd.clone.clone, body=%wide.region_59.60_spmd.clone.clone.sunk | while | flops 4228 | bytes 18367 | solution.py:78
  2016.5 45.0 %while.701 = (s32[]{:T(128)}, f32[32,32]{0,1:T(8,128)S(1)}, f32[32,32]{0,1:T(8,128)S(1)}, s32[]{:T(128)}, s32[]{:T(128)}, /*index=5*/s32[]{:T(128)}) while((s32[]{:T(128)}, f32[32,32]{0,1:T(8,128)S(1)}, f32[32,32]{0,1:T(8,128)S(1)}, s32[]{:T(128)}, s32[]{:T(128)}, /*index=5*/s32[]{:T(128)}) %tuple.1857), condition=%wide.region_62.63_spmd.clone.clone, body=%wide.region_61.62_spmd.clone.clone.sunk | while | flops 4292 | bytes 19003 | solution.py:60
  2061.5 43.6 %while.702 = (s32[]{:T(128)}, f32[32,32]{1,0:T(8,128)S(1)}, f32[32,32]{1,0:T(8,128)S(1)}, f32[32,32]{0,1:T(8,128)S(1)}, s32[]{:T(128)}, /*index=5*/s32[]{:T(128)}, s32[]{:T(128)}) while((s32[]{:T(128)}, f32[32,32]{1,0:T(8,128)S(1)}, f32[32,32]{1,0:T(8,128)S(1)}, f32[32,32]{0,1:T(8,128)S(1)}, s32[]{:T(128)}, ...), condition=%wide.region_64.65_spmd.clone.clone, body=%wide.region_63.64_spmd.clone.clone.sunk | while | flops 4228 | bytes 18367 | solution.py:78
  (5438 shorter events, 1352.4 us)
Async XLA Ops:
  7.2 538.7 %all-reduce.4.cloned.1.call-start = ((), (), s32[]{:S(2)}) async-start(), calls=%async_computation.1 | async-start | bytes 4194304 | tf_op jit(solution)/shard_map/psum | solution.py:159
  8.1 5.4 collective-permute-start
  12.1 4.4 collective-permute-start.1
  62.1 1.3 copy-start.15
  66.1 0.7 copy-start.24
  66.1 1.6 copy-start.16
  66.1 573.3 %copy-start = (f32[32,32]{1,0:T(8,128)}, f32[32,32]{1,0:T(8,128)S(1)}, u32[]{:S(2)}) copy-start(f32[32,32]{1,0:T(8,128)S(1)} %fusion.258) | copy-start | bytes 12292
  639.5 135.1 %copy-start.2 = (f32[32,32]{1,0:T(8,128)S(1)}, f32[32,32]{1,0:T(8,128)}, u32[]{:S(2)}) copy-start(f32[32,32]{1,0:T(8,128)} %copy-done) | copy-start | bytes 12292
  728.2 91.3 %copy-start.22 = (f32[32,32]{0,1:T(8,128)}, f32[32,32]{0,1:T(8,128)S(1)}, u32[]{:S(2)}) copy-start(f32[32,32]{0,1:T(8,128)S(1)} %get-tuple-element.7857) | copy-start | bytes 12292
  818.2 1.4 copy-start.21
  818.6 98.3 %copy-start.3 = (f32[32,32]{1,0:T(8,128)S(1)}, f32[32,32]{1,0:T(8,128)}, u32[]{:S(2)}) copy-start(f32[32,32]{1,0:T(8,128)} %copy-done) | copy-start | bytes 12292
  819.6 184.9 %copy-start.20 = (f32[32,32]{0,1:T(8,128)S(1)}, f32[32,32]{0,1:T(8,128)}, u32[]{:S(2)}) copy-start(f32[32,32]{0,1:T(8,128)} %custom-call.8) | copy-start | bytes 12292
  906.2 143.3 %copy-start.4 = (f32[32,32]{1,0:T(8,128)S(1)}, f32[32,32]{1,0:T(8,128)}, u32[]{:S(2)}) copy-start(f32[32,32]{1,0:T(8,128)} %copy-done) | copy-start | bytes 12292
  1003.3 90.8 %copy-start.19 = (f32[32,32]{0,1:T(8,128)S(1)}, f32[32,32]{0,1:T(8,128)}, u32[]{:S(2)}) copy-start(f32[32,32]{0,1:T(8,128)} %custom-call.10) | copy-start | bytes 12292
  1003.7 135.5 %copy-start.5 = (f32[32,32]{1,0:T(8,128)S(1)}, f32[32,32]{1,0:T(8,128)}, u32[]{:S(2)}) copy-start(f32[32,32]{1,0:T(8,128)} %copy-done) | copy-start | bytes 12292
  1093.1 90.7 %copy-start.18 = (f32[32,32]{0,1:T(8,128)S(1)}, f32[32,32]{0,1:T(8,128)}, u32[]{:S(2)}) copy-start(f32[32,32]{0,1:T(8,128)} %custom-call.12) | copy-start | bytes 12292
  1093.4 135.4 %copy-start.6 = (f32[32,32]{1,0:T(8,128)S(1)}, f32[32,32]{1,0:T(8,128)}, u32[]{:S(2)}) copy-start(f32[32,32]{1,0:T(8,128)} %copy-done) | copy-start | bytes 12292
  1139.2 134.2 %copy-start.17 = (f32[32,32]{0,1:T(8,128)S(1)}, f32[32,32]{0,1:T(8,128)}, u32[]{:S(2)}) copy-start(f32[32,32]{0,1:T(8,128)} %custom-call.14) | copy-start | bytes 12292
  1183.0 143.6 %copy-start.7 = (f32[32,32]{1,0:T(8,128)S(1)}, f32[32,32]{1,0:T(8,128)}, u32[]{:S(2)}) copy-start(f32[32,32]{1,0:T(8,128)} %copy-done) | copy-start | bytes 12292
  1272.7 143.4 %copy-start.8 = (f32[32,32]{1,0:T(8,128)S(1)}, f32[32,32]{1,0:T(8,128)}, u32[]{:S(2)}) copy-start(f32[32,32]{1,0:T(8,128)} %copy-done) | copy-start | bytes 12292
  1322.9 182.6 %copy-start.9 = (f32[32,32]{1,0:T(8,128)S(1)}, f32[32,32]{1,0:T(8,128)}, u32[]{:S(2)}) copy-start(f32[32,32]{1,0:T(8,128)} %copy-done) | copy-start | bytes 12292
  1371.0 223.8 %copy-start.10 = (f32[32,32]{1,0:T(8,128)S(1)}, f32[32,32]{1,0:T(8,128)}, u32[]{:S(2)}) copy-start(f32[32,32]{1,0:T(8,128)} %copy-done) | copy-start | bytes 12292
  1505.5 186.3 %copy-start.11 = (f32[32,32]{1,0:T(8,128)S(1)}, f32[32,32]{1,0:T(8,128)}, u32[]{:S(2)}) copy-start(f32[32,32]{1,0:T(8,128)} %copy-done) | copy-start | bytes 12292
  1549.8 231.2 %copy-start.12 = (f32[32,32]{1,0:T(8,128)S(1)}, f32[32,32]{1,0:T(8,128)}, u32[]{:S(2)}) copy-start(f32[32,32]{1,0:T(8,128)} %copy-done) | copy-start | bytes 12292
  1638.7 231.5 %copy-start.13 = (f32[32,32]{1,0:T(8,128)S(1)}, f32[32,32]{1,0:T(8,128)}, u32[]{:S(2)}) copy-start(f32[32,32]{1,0:T(8,128)} %copy-done) | copy-start | bytes 12292
  1691.8 267.6 %copy-start.14 = (f32[32,32]{1,0:T(8,128)S(1)}, f32[32,32]{1,0:T(8,128)}, u32[]{:S(2)}) copy-start(f32[32,32]{1,0:T(8,128)} %copy-done) | copy-start | bytes 12292
  1913.8 102.7 %copy-start.23 = (f32[32,32]{0,1:T(8,128)S(1)}, f32[32,32]{0,1:T(8,128)}, u32[]{:S(2)}) copy-start(f32[32,32]{0,1:T(8,128)} %custom-call.30) | copy-start | bytes 12292
  1959.4 102.1 %copy-start.1 = (f32[32,32]{1,0:T(8,128)S(1)}, f32[32,32]{1,0:T(8,128)}, u32[]{:S(2)}) copy-start(f32[32,32]{1,0:T(8,128)} %copy-done) | copy-start | bytes 12292
  2133.2 0.7 copy-start.25
Sparse Core Ops, SparseCore 0:
  66.2 479.6 all-reduce.3
where the time goes:
time: 2160 us; the launch traced here: 2140 us
  local copies, waits for them, and re-layouts  667 us (31%)
  other arithmetic  500 us (23%)
  loops' own time  382 us (18%)
  waiting for transfers between devices  371 us (17%)
  blocking collectives  144 us (7%)
  matrix products  56.1 us (3%)
    another operation x16, loops' own time, small_factor(): lax.fori_loop(0, order, column_step, (matrix, jnp.zeros_like(matrix)))[1]  369 us
    psum x1, waiting for transfers between devices, shards(): gram_block, projected = lax.psum((gram_block, projected), ('rows', 'cols'))  368 us
    mul x1024, other arithmetic, row_step(): rest = rest - below[:, None] * value  363 us
    dynamic_slice x512, local copies, waits for them, and re-layouts, row_step(): pivot = lax.dynamic_slice_in_dim(column, index_row, 1, 0)[0]  322 us
    dynamic_slice x512, local copies, waits for them, and re-layouts, column_step(): pivot = jnp.sqrt(lax.dynamic_slice_in_dim(column, index_col, 1, 0)[0])  301 us
    psum x1, blocking collectives, shards(): gram_block, projected = lax.psum((gram_block, projected), ('rows', 'cols'))  110 us
    select_n x512, other arithmetic, column_step(): lower = jnp.where(positions[None, :] == index_col, column[:, None], lower)  80.9 us
    dot_general x123, matrix products, matmul(): jnp.dot(left, right, precision=lax.Precision.HIGHEST, preferred_element_t...  46.5 us

commit v1 on v0

--- a/solution.py
+++ b/solution.py
@@ -1,3 +1,4 @@
+import functools
 import math
 import jax
 import jax.numpy as jnp
@@ -6,6 +7,13 @@
 
 TILE = 128
 PW = 256
+
+
+def extend_the_edge(arr_in, axis_id, peer_axis):
+    return jax.lax.psum(jax.lax.psum(arr_in, axis_name=axis_id), peer_axis)
+
+
+panels_choose = functools.partial(extend_the_edge, axis_id="rows", peer_axis="cols")
 
 
 def padded_2(cells, sides, width):
@@ -156,7 +164,7 @@
         leading, row_major, (((0,), (0,)), ((), ())), preferred_element_type=jnp.float32
     )
     projected = jnp.dot(grad_part, leading, preferred_element_type=jnp.float32)
-    gram_block, projected = lax.psum((gram_block, projected), ("rows", "cols"))
+    gram_block, projected = panels_choose((gram_block, projected))
     gram_head = gram_block[:, :factored]
     gram_own = lax.dynamic_slice_in_dim(
         gram_block, lax.axis_index("cols") * cols_here, cols_here, 1

time: 2160 us -> 2110 us (0.977)
  waiting for transfers between devices: 371 us -> 276 us
  blocking collectives: 144 us -> 197 us
    psum x1 -> x2, waiting for transfers between devices: 368 us -> 273 us  [extend_the_edge(): return jax.lax.psum(jax.lax.psum(arr_in, axis_name=axis_id), peer_axis)]
    psum x1 -> x2, blocking collectives: 110 us -> 162 us  [extend_the_edge(): return jax.lax.psum(jax.lax.psum(arr_in, axis_name=axis_id), peer_axis)]
where the time goes in v1:
time: 2110 us; the launch traced here: 2100 us
  local copies, waits for them, and re-layouts  667 us (32%)
  other arithmetic  500 us (24%)
  loops' own time  383 us (18%)
  waiting for transfers between devices  276 us (13%)
  blocking collectives  197 us (9%)
  matrix products  56.1 us (3%)
    another operation x16, loops' own time, small_factor(): lax.fori_loop(0, order, column_step, (matrix, jnp.zeros_like(matrix)))[1]  370 us
    mul x1024, other arithmetic, row_step(): rest = rest - below[:, None] * value  363 us
    dynamic_slice x512, local copies, waits for them, and re-layouts, row_step(): pivot = lax.dynamic_slice_in_dim(column, index_row, 1, 0)[0]  322 us
    dynamic_slice x512, local copies, waits for them, and re-layouts, column_step(): pivot = jnp.sqrt(lax.dynamic_slice_in_dim(column, index_col, 1, 0)[0])  302 us
    psum x2, waiting for transfers between devices, extend_the_edge(): return jax.lax.psum(jax.lax.psum(arr_in, axis_name=axis_id), peer_axis)  273 us
    psum x2, blocking collectives, extend_the_edge(): return jax.lax.psum(jax.lax.psum(arr_in, axis_name=axis_id), peer_axis)  162 us
    select_n x512, other arithmetic, column_step(): lower = jnp.where(positions[None, :] == index_col, column[:, None], lower)  80.8 us
    dot_general x123, matrix products, matmul(): jnp.dot(left, right, precision=lax.Precision.HIGHEST, preferred_element_t...  46.5 us

profile of v1, /device:TPU:1, one launch (start us, length us, event | category | flops | bytes accessed | tf_op | source)
XLA Modules:
  0.0 2099.4 jit_solution(10871177124091725457)
XLA Ops:
  66.1 272.9 %all-reduce.5.cloned.1.call-done = f32[512,1024]{1,0:T(8,128)} async-done(((f32[512,1024]{1,0:T(8,128)}), f32[512,1024]{1,0:T(8,128)}) %all-reduce.5.cloned.1.call-update) | async-done | bytes 2097168 | tf_op jit(solution)/shard_map/psum | solution.py:13
  339.8 112.5 %psum.30 = f32[512]{0:T(512)S(1)} all-reduce(f32[512]{0:T(512)S(1)} %bitcast.1236), channel_id=1, replica_groups=mesh['rows'=64,'cols'=8] {'rows'}, use_global_device_ids=true, to_apply=%region_66.67 | all-reduce | flops 512 | bytes 4096 | tf_op jit(solution)/shard_map/psum | solution.py:13
  452.4 49.8 %psum.31 = f32[512]{0:T(512)S(1)} all-reduce(f32[512]{0:T(512)S(1)} %psum.30), channel_id=1, replica_groups=mesh['rows'=64,'cols'=8] {'cols'}, use_global_device_ids=true, to_apply=%region_67.68 | all-reduce | flops 512 | bytes 4096 | tf_op jit(solution)/shard_map/psum | solution.py:13
  503.0 47.9 %while.671 = (s32[]{:T(128)}, f32[32,32]{0,1:T(8,128)S(1)}, f32[32,32]{0,1:T(8,128)S(1)}, s32[]{:T(128)}, s32[]{:T(128)}, /*index=5*/s32[]{:T(128)}) while((s32[]{:T(128)}, f32[32,32]{0,1:T(8,128)S(1)}, f32[32,32]{0,1:T(8,128)S(1)}, s32[]{:T(128)}, s32[]{:T(128)}, /*index=5*/s32[]{:T(128)}) %tuple.1741), condition=%wide.region_3.4_spmd.clone.clone, body=%wide.region_2.3_spmd.clone.clone.sunk | while | flops 4292 | bytes 19003 | solution.py:68
  598.3 45.0 %while.673 = (s32[]{:T(128)}, f32[32,32]{0,1:T(8,128)S(1)}, f32[32,32]{0,1:T(8,128)S(1)}, s32[]{:T(128)}, s32[]{:T(128)}, /*index=5*/s32[]{:T(128)}) while((s32[]{:T(128)}, f32[32,32]{0,1:T(8,128)S(1)}, f32[32,32]{0,1:T(8,128)S(1)}, s32[]{:T(128)}, s32[]{:T(128)}, /*index=5*/s32[]{:T(128)}) %tuple.1747), condition=%wide.region_7.8_spmd.clone.clone, body=%wide.region_6.7_spmd.clone.clone.sunk | while | flops 4292 | bytes 19003 | solution.py:68
  688.3 45.0 %while.675 = (s32[]{:T(128)}, f32[32,32]{0,1:T(8,128)S(1)}, f32[32,32]{0,1:T(8,128)S(1)}, s32[]{:T(128)}, s32[]{:T(128)}, /*index=5*/s32[]{:T(128)}) while((s32[]{:T(128)}, f32[32,32]{0,1:T(8,128)S(1)}, f32[32,32]{0,1:T(8,128)S(1)}, s32[]{:T(128)}, s32[]{:T(128)}, /*index=5*/s32[]{:T(128)}) %tuple.1753), condition=%wide.region_11.12_spmd.clone.clone, body=%wide.region_10.11_spmd.clone.clone.sunk | while | flops 4292 | bytes 19003 | solution.py:68
  733.3 43.6 %while.676 = (s32[]{:T(128)}, f32[32,32]{1,0:T(8,128)S(1)}, f32[32,32]{1,0:T(8,128)S(1)}, f32[32,32]{0,1:T(8,128)S(1)}, s32[]{:T(128)}, /*index=5*/s32[]{:T(128)}, s32[]{:T(128)}) while((s32[]{:T(128)}, f32[32,32]{1,0:T(8,128)S(1)}, f32[32,32]{1,0:T(8,128)S(1)}, f32[32,32]{0,1:T(8,128)S(1)}, s32[]{:T(128)}, ...), condition=%wide.region_13.14_spmd.clone.clone, body=%wide.region_12.13_spmd.clone.clone.sunk | while | flops 4228 | bytes 18367 | solution.py:86
  778.3 86.5 %while.677 = (s32[]{:T(128)}, f32[32,32]{0,1:T(8,128)S(1)}, f32[32,32]{0,1:T(8,128)}, s32[]{:T(128)}, s32[]{:T(128)}, /*index=5*/s32[]{:T(128)}) while((s32[]{:T(128)}, f32[32,32]{0,1:T(8,128)S(1)}, f32[32,32]{0,1:T(8,128)}, s32[]{:T(128)}, s32[]{:T(128)}, /*index=5*/s32[]{:T(128)}) %tuple.1759), condition=%wide.region_15.16_spmd.clone.clone, body=%wide.region_14.15_spmd.clone.clone.sunk | while | flops 4292 | bytes 19003 | solution.py:68
  875.6 86.4 %while.678 = (s32[]{:T(128)}, f32[32,32]{1,0:T(8,128)S(1)}, f32[32,32]{1,0:T(8,128)S(1)}, f32[32,32]{0,1:T(8,128)}, s32[]{:T(128)}, /*index=5*/s32[]{:T(128)}, s32[]{:T(128)}) while((s32[]{:T(128)}, f32[32,32]{1,0:T(8,128)S(1)}, f32[32,32]{1,0:T(8,128)S(1)}, f32[32,32]{0,1:T(8,128)}, s32[]{:T(128)}, ...), condition=%wide.region_17.18_spmd.clone.clone, body=%wide.region_16.17_spmd.clone.clone.sunk | while | flops 4228 | bytes 18751 | solution.py:86
  963.1 45.0 %while.679 = (s32[]{:T(128)}, f32[32,32]{0,1:T(8,128)S(1)}, f32[32,32]{0,1:T(8,128)S(1)}, s32[]{:T(128)}, s32[]{:T(128)}, /*index=5*/s32[]{:T(128)}) while((s32[]{:T(128)}, f32[32,32]{0,1:T(8,128)S(1)}, f32[32,32]{0,1:T(8,128)S(1)}, s32[]{:T(128)}, s32[]{:T(128)}, /*index=5*/s32[]{:T(128)}) %tuple.1858), condition=%wide.region_19.20_spmd.clone.clone, body=%wide.region_18.19_spmd.clone.clone.sunk | while | flops 4292 | bytes 19003 | solution.py:68
  1008.1 43.6 %while.680 = (s32[]{:T(128)}, f32[32,32]{1,0:T(8,128)S(1)}, f32[32,32]{1,0:T(8,128)S(1)}, f32[32,32]{0,1:T(8,128)S(1)}, s32[]{:T(128)}, /*index=5*/s32[]{:T(128)}, s32[]{:T(128)}) while((s32[]{:T(128)}, f32[32,32]{1,0:T(8,128)S(1)}, f32[32,32]{1,0:T(8,128)S(1)}, f32[32,32]{0,1:T(8,128)S(1)}, s32[]{:T(128)}, ...), condition=%wide.region_21.22_spmd.clone.clone, body=%wide.region_20.21_spmd.clone.clone.sunk | while | flops 4228 | bytes 18367 | solution.py:86
  1052.8 45.0 %while.681 = (s32[]{:T(128)}, f32[32,32]{0,1:T(8,128)S(1)}, f32[32,32]{0,1:T(8,128)S(1)}, s32[]{:T(128)}, s32[]{:T(128)}, /*index=5*/s32[]{:T(128)}) while((s32[]{:T(128)}, f32[32,32]{0,1:T(8,128)S(1)}, f32[32,32]{0,1:T(8,128)S(1)}, s32[]{:T(128)}, s32[]{:T(128)}, /*index=5*/s32[]{:T(128)}) %tuple.1857), condition=%wide.region_23.24_spmd.clone.clone, body=%wide.region_22.23_spmd.clone.clone.sunk | while | flops 4292 | bytes 19003 | solution.py:68
  1097.8 43.6 %while.682 = (s32[]{:T(128)}, f32[32,32]{1,0:T(8,128)S(1)}, f32[32,32]{1,0:T(8,128)S(1)}, f32[32,32]{0,1:T(8,128)S(1)}, s32[]{:T(128)}, /*index=5*/s32[]{:T(128)}, s32[]{:T(128)}) while((s32[]{:T(128)}, f32[32,32]{1,0:T(8,128)S(1)}, f32[32,32]{1,0:T(8,128)S(1)}, f32[32,32]{0,1:T(8,128)S(1)}, s32[]{:T(128)}, ...), condition=%wide.region_25.26_spmd.clone.clone, body=%wide.region_24.25_spmd.clone.clone.sunk | while | flops 4228 | bytes 18367 | solution.py:86
  1142.4 45.0 %while.683 = (s32[]{:T(128)}, f32[32,32]{0,1:T(8,128)S(1)}, f32[32,32]{0,1:T(8,128)S(1)}, s32[]{:T(128)}, s32[]{:T(128)}, /*index=5*/s32[]{:T(128)}) while((s32[]{:T(128)}, f32[32,32]{0,1:T(8,128)S(1)}, f32[32,32]{0,1:T(8,128)S(1)}, s32[]{:T(128)}, s32[]{:T(128)}, /*index=5*/s32[]{:T(128)}) %tuple.1856), condition=%wide.region_27.28_spmd.clone.clone, body=%wide.region_26.27_spmd.clone.clone.sunk | while | flops 4292 | bytes 19003 | solution.py:68
  1187.4 43.6 %while.684 = (s32[]{:T(128)}, f32[32,32]{1,0:T(8,128)S(1)}, f32[32,32]{1,0:T(8,128)S(1)}, f32[32,32]{0,1:T(8,128)S(1)}, s32[]{:T(128)}, /*index=5*/s32[]{:T(128)}, s32[]{:T(128)}) while((s32[]{:T(128)}, f32[32,32]{1,0:T(8,128)S(1)}, f32[32,32]{1,0:T(8,128)S(1)}, f32[32,32]{0,1:T(8,128)S(1)}, s32[]{:T(128)}, ...), condition=%wide.region_29.30_spmd.clone.clone, body=%wide.region_28.29_spmd.clone.clone.sunk | while | flops 4228 | bytes 18367 | solution.py:86
  1232.0 45.0 %while.685 = (s32[]{:T(128)}, f32[32,32]{0,1:T(8,128)S(1)}, f32[32,32]{0,1:T(8,128)S(1)}, s32[]{:T(128)}, s32[]{:T(128)}, /*index=5*/s32[]{:T(128)}) while((s32[]{:T(128)}, f32[32,32]{0,1:T(8,128)S(1)}, f32[32,32]{0,1:T(8,128)S(1)}, s32[]{:T(128)}, s32[]{:T(128)}, /*index=5*/s32[]{:T(128)}) %tuple.1855), condition=%wide.region_31.32_spmd.clone.clone, body=%wide.region_30.31_spmd.clone.clone.sunk | while | flops 4292 | bytes 19003 | solution.py:68
  1285.3 43.6 %while.686 = (s32[]{:T(128)}, f32[32,32]{1,0:T(8,128)S(1)}, f32[32,32]{1,0:T(8,128)S(1)}, f32[32,32]{0,1:T(8,128)S(1)}, s32[]{:T(128)}, /*index=5*/s32[]{:T(128)}, s32[]{:T(128)}) while((s32[]{:T(128)}, f32[32,32]{1,0:T(8,128)S(1)}, f32[32,32]{1,0:T(8,128)S(1)}, f32[32,32]{0,1:T(8,128)S(1)}, s32[]{:T(128)}, ...), condition=%wide.region_33.34_spmd.clone.clone, body=%wide.region_32.33_spmd.clone.clone.sunk | while | flops 4228 | bytes 18367 | solution.py:86
  1329.6 45.0 %while.687 = (s32[]{:T(128)}, f32[32,32]{0,1:T(8,128)S(1)}, f32[32,32]{0,1:T(8,128)S(1)}, s32[]{:T(128)}, s32[]{:T(128)}, /*index=5*/s32[]{:T(128)}) while((s32[]{:T(128)}, f32[32,32]{0,1:T(8,128)S(1)}, f32[32,32]{0,1:T(8,128)S(1)}, s32[]{:T(128)}, s32[]{:T(128)}, /*index=5*/s32[]{:T(128)}) %tuple.1789), condition=%wide.region_35.36_spmd.clone.clone, body=%wide.region_34.35_spmd.clone.clone.sunk | while | flops 4292 | bytes 19003 | solution.py:68
  1419.1 45.0 %while.689 = (s32[]{:T(128)}, f32[32,32]{0,1:T(8,128)S(1)}, f32[32,32]{0,1:T(8,128)S(1)}, s32[]{:T(128)}, s32[]{:T(128)}, /*index=5*/s32[]{:T(128)}) while((s32[]{:T(128)}, f32[32,32]{0,1:T(8,128)S(1)}, f32[32,32]{0,1:T(8,128)S(1)}, s32[]{:T(128)}, s32[]{:T(128)}, /*index=5*/s32[]{:T(128)}) %tuple.1795), condition=%wide.region_39.40_spmd.clone.clone, body=%wide.region_38.39_spmd.clone.clone.sunk | while | flops 4292 | bytes 19003 | solution.py:68
  1464.1 43.6 %while.690 = (s32[]{:T(128)}, f32[32,32]{1,0:T(8,128)S(1)}, f32[32,32]{1,0:T(8,128)S(1)}, f32[32,32]{0,1:T(8,128)S(1)}, s32[]{:T(128)}, /*index=5*/s32[]{:T(128)}, s32[]{:T(128)}) while((s32[]{:T(128)}, f32[32,32]{1,0:T(8,128)S(1)}, f32[32,32]{1,0:T(8,128)S(1)}, f32[32,32]{0,1:T(8,128)S(1)}, s32[]{:T(128)}, ...), condition=%wide.region_41.42_spmd.clone.clone, body=%wide.region_40.41_spmd.clone.clone.sunk | while | flops 4228 | bytes 18367 | solution.py:86
  1508.4 45.0 %while.691 = (s32[]{:T(128)}, f32[32,32]{0,1:T(8,128)S(1)}, f32[32,32]{0,1:T(8,128)S(1)}, s32[]{:T(128)}, s32[]{:T(128)}, /*index=5*/s32[]{:T(128)}) while((s32[]{:T(128)}, f32[32,32]{0,1:T(8,128)S(1)}, f32[32,32]{0,1:T(8,128)S(1)}, s32[]{:T(128)}, s32[]{:T(128)}, /*index=5*/s32[]{:T(128)}) %tuple.1801), condition=%wide.region_43.44_spmd.clone.clone, body=%wide.region_42.43_spmd.clone.clone.sunk | while | flops 4292 | bytes 19003 | solution.py:68
  1553.5 43.6 %while.692 = (s32[]{:T(128)}, f32[32,32]{1,0:T(8,128)S(1)}, f32[32,32]{1,0:T(8,128)S(1)}, f32[32,32]{0,1:T(8,128)S(1)}, s32[]{:T(128)}, /*index=5*/s32[]{:T(128)}, s32[]{:T(128)}) while((s32[]{:T(128)}, f32[32,32]{1,0:T(8,128)S(1)}, f32[32,32]{1,0:T(8,128)S(1)}, f32[32,32]{0,1:T(8,128)S(1)}, s32[]{:T(128)}, ...), condition=%wide.region_45.46_spmd.clone.clone, body=%wide.region_44.45_spmd.clone.clone.sunk | while | flops 4228 | bytes 18367 | solution.py:86
  1597.8 45.0 %while.693 = (s32[]{:T(128)}, f32[32,32]{0,1:T(8,128)S(1)}, f32[32,32]{0,1:T(8,128)S(1)}, s32[]{:T(128)}, s32[]{:T(128)}, /*index=5*/s32[]{:T(128)}) while((s32[]{:T(128)}, f32[32,32]{0,1:T(8,128)S(1)}, f32[32,32]{0,1:T(8,128)S(1)}, s32[]{:T(128)}, s32[]{:T(128)}, /*index=5*/s32[]{:T(128)}) %tuple.1807), condition=%wide.region_47.48_spmd.clone.clone, body=%wide.region_46.47_spmd.clone.clone.sunk | while | flops 4292 | bytes 19003 | solution.py:68
  1650.4 43.6 %while.694 = (s32[]{:T(128)}, f32[32,32]{1,0:T(8,128)S(1)}, f32[32,32]{1,0:T(8,128)S(1)}, f32[32,32]{0,1:T(8,128)S(1)}, s32[]{:T(128)}, /*index=5*/s32[]{:T(128)}, s32[]{:T(128)}) while((s32[]{:T(128)}, f32[32,32]{1,0:T(8,128)S(1)}, f32[32,32]{1,0:T(8,128)S(1)}, f32[32,32]{0,1:T(8,128)S(1)}, s32[]{:T(128)}, ...), condition=%wide.region_49.50_spmd.clone.clone, body=%wide.region_48.49_spmd.clone.clone.sunk | while | flops 4228 | bytes 18367 | solution.py:86
  1694.6 45.0 %while.695 = (s32[]{:T(128)}, f32[32,32]{0,1:T(8,128)S(1)}, f32[32,32]{0,1:T(8,128)S(1)}, s32[]{:T(128)}, s32[]{:T(128)}, /*index=5*/s32[]{:T(128)}) while((s32[]{:T(128)}, f32[32,32]{0,1:T(8,128)S(1)}, f32[32,32]{0,1:T(8,128)S(1)}, s32[]{:T(128)}, s32[]{:T(128)}, /*index=5*/s32[]{:T(128)}) %tuple.1813), condition=%wide.region_51.52_spmd.clone.clone, body=%wide.region_50.51_spmd.clone.clone.sunk | while | flops 4292 | bytes 19003 | solution.py:68
  1739.6 43.6 %while.696 = (s32[]{:T(128)}, f32[32,32]{1,0:T(8,128)S(1)}, f32[32,32]{1,0:T(8,128)S(1)}, f32[32,32]{0,1:T(8,128)S(1)}, s32[]{:T(128)}, /*index=5*/s32[]{:T(128)}, s32[]{:T(128)}) while((s32[]{:T(128)}, f32[32,32]{1,0:T(8,128)S(1)}, f32[32,32]{1,0:T(8,128)S(1)}, f32[32,32]{0,1:T(8,128)S(1)}, s32[]{:T(128)}, ...), condition=%wide.region_53.54_spmd.clone.clone, body=%wide.region_52.53_spmd.clone.clone.sunk | while | flops 4228 | bytes 18367 | solution.py:86
  1783.8 45.0 %while.697 = (s32[]{:T(128)}, f32[32,32]{0,1:T(8,128)S(1)}, f32[32,32]{0,1:T(8,128)S(1)}, s32[]{:T(128)}, s32[]{:T(128)}, /*index=5*/s32[]{:T(128)}) while((s32[]{:T(128)}, f32[32,32]{0,1:T(8,128)S(1)}, f32[32,32]{0,1:T(8,128)S(1)}, s32[]{:T(128)}, s32[]{:T(128)}, /*index=5*/s32[]{:T(128)}) %tuple.1819), condition=%wide.region_55.56_spmd.clone.clone, body=%wide.region_54.55_spmd.clone.clone.sunk | while | flops 4292 | bytes 19003 | solution.py:68
  1828.8 43.6 %while.698 = (s32[]{:T(128)}, f32[32,32]{1,0:T(8,128)S(1)}, f32[32,32]{1,0:T(8,128)S(1)}, f32[32,32]{0,1:T(8,128)S(1)}, s32[]{:T(128)}, /*index=5*/s32[]{:T(128)}, s32[]{:T(128)}) while((s32[]{:T(128)}, f32[32,32]{1,0:T(8,128)S(1)}, f32[32,32]{1,0:T(8,128)S(1)}, f32[32,32]{0,1:T(8,128)S(1)}, s32[]{:T(128)}, ...), condition=%wide.region_57.58_spmd.clone.clone, body=%wide.region_56.57_spmd.clone.clone.sunk | while | flops 4228 | bytes 18367 | solution.py:86
  1873.0 45.0 %while.699 = (s32[]{:T(128)}, f32[32,32]{0,1:T(8,128)S(1)}, f32[32,32]{0,1:T(8,128)S(1)}, s32[]{:T(128)}, s32[]{:T(128)}, /*index=5*/s32[]{:T(128)}) while((s32[]{:T(128)}, f32[32,32]{0,1:T(8,128)S(1)}, f32[32,32]{0,1:T(8,128)S(1)}, s32[]{:T(128)}, s32[]{:T(128)}, /*index=5*/s32[]{:T(128)}) %tuple.1825), condition=%wide.region_59.60_spmd.clone.clone, body=%wide.region_58.59_spmd.clone.clone.sunk | while | flops 4292 | bytes 19003 | solution.py:68
  1918.0 43.6 %while.700 = (s32[]{:T(128)}, f32[32,32]{1,0:T(8,128)S(1)}, f32[32,32]{1,0:T(8,128)S(1)}, f32[32,32]{0,1:T(8,128)S(1)}, s32[]{:T(128)}, /*index=5*/s32[]{:T(128)}, s32[]{:T(128)}) while((s32[]{:T(128)}, f32[32,32]{1,0:T(8,128)S(1)}, f32[32,32]{1,0:T(8,128)S(1)}, f32[32,32]{0,1:T(8,128)S(1)}, s32[]{:T(128)}, ...), condition=%wide.region_61.62_spmd.clone.clone, body=%wide.region_60.61_spmd.clone.clone.sunk | while | flops 4228 | bytes 18367 | solution.py:86
  1975.1 45.0 %while.701 = (s32[]{:T(128)}, f32[32,32]{0,1:T(8,128)S(1)}, f32[32,32]{0,1:T(8,128)S(1)}, s32[]{:T(128)}, s32[]{:T(128)}, /*index=5*/s32[]{:T(128)}) while((s32[]{:T(128)}, f32[32,32]{0,1:T(8,128)S(1)}, f32[32,32]{0,1:T(8,128)S(1)}, s32[]{:T(128)}, s32[]{:T(128)}, /*index=5*/s32[]{:T(128)}) %tuple.1859), condition=%wide.region_63.64_spmd.clone.clone, body=%wide.region_62.63_spmd.clone.clone.sunk | while | flops 4292 | bytes 19003 | solution.py:68
  2020.1 43.6 %while.702 = (s32[]{:T(128)}, f32[32,32]{1,0:T(8,128)S(1)}, f32[32,32]{1,0:T(8,128)S(1)}, f32[32,32]{0,1:T(8,128)S(1)}, s32[]{:T(128)}, /*index=5*/s32[]{:T(128)}, s32[]{:T(128)}) while((s32[]{:T(128)}, f32[32,32]{1,0:T(8,128)S(1)}, f32[32,32]{1,0:T(8,128)S(1)}, f32[32,32]{0,1:T(8,128)S(1)}, s32[]{:T(128)}, ...), condition=%wide.region_65.66_spmd.clone.clone, body=%wide.region_64.65_spmd.clone.clone.sunk | while | flops 4228 | bytes 18367 | solution.py:86
  (5442 shorter events, 1395.9 us)
Async XLA Ops:
  7.2 331.9 %all-reduce.5.cloned.1.call-start = ((), (), s32[]{:S(2)}) async-start(), calls=%async_computation.1 | async-start | bytes 4194304 | tf_op jit(solution)/shard_map/psum | solution.py:13
  8.1 5.4 collective-permute-start
  12.1 4.4 collective-permute-start.1
  62.1 1.3 copy-start.15
  66.0 273.4 %copy-start.24 = (bf16[8,1024]{1,0:T(8,128)(2,1)S(1)}, bf16[8,1024]{1,0:T(8,128)(2,1)}, u32[]{:S(2)}) copy-start(bf16[8,1024]{1,0:T(8,128)(2,1)} %param.133) | copy-start | bytes 49156
  66.0 273.4 %copy-start.16 = (bf16[8,1024,128]{1,2,0:T(8,128)(2,1)S(1)}, bf16[8,1024,128]{1,2,0:T(8,128)(2,1)}, u32[]{:S(2)}) copy-start(bf16[8,1024,128]{1,2,0:T(8,128)(2,1)} %copy-done.15) | copy-start | bytes 6291460
  66.1 436.1 %all-reduce.7.cloned.1.call-start = ((), (), s32[]{:S(2)}) async-start(), calls=%async_computation.2 | async-start | bytes 4194304 | tf_op jit(solution)/shard_map/psum | solution.py:13
  339.1 259.1 %copy-start = (f32[32,32]{1,0:T(8,128)}, f32[32,32]{1,0:T(8,128)S(1)}, u32[]{:S(2)}) copy-start(f32[32,32]{1,0:T(8,128)S(1)} %fusion.258) | copy-start | bytes 12292
  598.2 135.1 %copy-start.2 = (f32[32,32]{1,0:T(8,128)S(1)}, f32[32,32]{1,0:T(8,128)}, u32[]{:S(2)}) copy-start(f32[32,32]{1,0:T(8,128)} %copy-done) | copy-start | bytes 12292
  686.9 91.3 %copy-start.22 = (f32[32,32]{0,1:T(8,128)}, f32[32,32]{0,1:T(8,128)S(1)}, u32[]{:S(2)}) copy-start(f32[32,32]{0,1:T(8,128)S(1)} %get-tuple-element.7861) | copy-start | bytes 12292
  776.9 1.4 copy-start.21
  777.3 98.2 %copy-start.3 = (f32[32,32]{1,0:T(8,128)S(1)}, f32[32,32]{1,0:T(8,128)}, u32[]{:S(2)}) copy-start(f32[32,32]{1,0:T(8,128)} %copy-done) | copy-start | bytes 12292
  778.3 184.8 %copy-start.20 = (f32[32,32]{0,1:T(8,128)S(1)}, f32[32,32]{0,1:T(8,128)}, u32[]{:S(2)}) copy-start(f32[32,32]{0,1:T(8,128)} %custom-call.8) | copy-start | bytes 12292
  864.9 143.2 %copy-start.4 = (f32[32,32]{1,0:T(8,128)S(1)}, f32[32,32]{1,0:T(8,128)}, u32[]{:S(2)}) copy-start(f32[32,32]{1,0:T(8,128)} %copy-done) | copy-start | bytes 12292
  962.0 90.8 %copy-start.19 = (f32[32,32]{0,1:T(8,128)S(1)}, f32[32,32]{0,1:T(8,128)}, u32[]{:S(2)}) copy-start(f32[32,32]{0,1:T(8,128)} %custom-call.10) | copy-start | bytes 12292
  962.3 135.5 %copy-start.5 = (f32[32,32]{1,0:T(8,128)S(1)}, f32[32,32]{1,0:T(8,128)}, u32[]{:S(2)}) copy-start(f32[32,32]{1,0:T(8,128)} %copy-done) | copy-start | bytes 12292
  1051.7 90.7 %copy-start.18 = (f32[32,32]{0,1:T(8,128)S(1)}, f32[32,32]{0,1:T(8,128)}, u32[]{:S(2)}) copy-start(f32[32,32]{0,1:T(8,128)} %custom-call.12) | copy-start | bytes 12292
  1052.0 135.4 %copy-start.6 = (f32[32,32]{1,0:T(8,128)S(1)}, f32[32,32]{1,0:T(8,128)}, u32[]{:S(2)}) copy-start(f32[32,32]{1,0:T(8,128)} %copy-done) | copy-start | bytes 12292
  1097.8 134.2 %copy-start.17 = (f32[32,32]{0,1:T(8,128)S(1)}, f32[32,32]{0,1:T(8,128)}, u32[]{:S(2)}) copy-start(f32[32,32]{0,1:T(8,128)} %custom-call.14) | copy-start | bytes 12292
  1141.7 143.6 %copy-start.7 = (f32[32,32]{1,0:T(8,128)S(1)}, f32[32,32]{1,0:T(8,128)}, u32[]{:S(2)}) copy-start(f32[32,32]{1,0:T(8,128)} %copy-done) | copy-start | bytes 12292
  1231.3 143.4 %copy-start.8 = (f32[32,32]{1,0:T(8,128)S(1)}, f32[32,32]{1,0:T(8,128)}, u32[]{:S(2)}) copy-start(f32[32,32]{1,0:T(8,128)} %copy-done) | copy-start | bytes 12292
  1281.5 182.6 %copy-start.9 = (f32[32,32]{1,0:T(8,128)S(1)}, f32[32,32]{1,0:T(8,128)}, u32[]{:S(2)}) copy-start(f32[32,32]{1,0:T(8,128)} %copy-done) | copy-start | bytes 12292
  1329.6 223.8 %copy-start.10 = (f32[32,32]{1,0:T(8,128)S(1)}, f32[32,32]{1,0:T(8,128)}, u32[]{:S(2)}) copy-start(f32[32,32]{1,0:T(8,128)} %copy-done) | copy-start | bytes 12292
  1464.1 186.3 %copy-start.11 = (f32[32,32]{1,0:T(8,128)S(1)}, f32[32,32]{1,0:T(8,128)}, u32[]{:S(2)}) copy-start(f32[32,32]{1,0:T(8,128)} %copy-done) | copy-start | bytes 12292
  1508.4 231.2 %copy-start.12 = (f32[32,32]{1,0:T(8,128)S(1)}, f32[32,32]{1,0:T(8,128)}, u32[]{:S(2)}) copy-start(f32[32,32]{1,0:T(8,128)} %copy-done) | copy-start | bytes 12292
  1597.4 231.5 %copy-start.13 = (f32[32,32]{1,0:T(8,128)S(1)}, f32[32,32]{1,0:T(8,128)}, u32[]{:S(2)}) copy-start(f32[32,32]{1,0:T(8,128)} %copy-done) | copy-start | bytes 12292
  1650.4 267.6 %copy-start.14 = (f32[32,32]{1,0:T(8,128)S(1)}, f32[32,32]{1,0:T(8,128)}, u32[]{:S(2)}) copy-start(f32[32,32]{1,0:T(8,128)} %copy-done) | copy-start | bytes 12292
  1872.4 102.7 %copy-start.23 = (f32[32,32]{0,1:T(8,128)S(1)}, f32[32,32]{0,1:T(8,128)}, u32[]{:S(2)}) copy-start(f32[32,32]{0,1:T(8,128)} %custom-call.30) | copy-start | bytes 12292
  1918.0 102.1 %copy-start.1 = (f32[32,32]{1,0:T(8,128)S(1)}, f32[32,32]{1,0:T(8,128)}, u32[]{:S(2)}) copy-start(f32[32,32]{1,0:T(8,128)} %copy-done) | copy-start | bytes 12292
  2091.8 0.7 copy-start.25
Sparse Core Ops, SparseCore 0:
  66.2 272.8 all-reduce.4
  341.5 83.6 all-reduce.6
